TPU v7x, 32 devices: a whole 2x2x4 slice. The times are simulated.
32 devices in a mesh: row: 4 (over y, x), col: 8 (over z, core).
Axes of the slice: x: 2, y: 2, z: 4, core: 2. Of those that a mesh axis runs over, the one named last changes fastest.
Arguments:
- points: bfloat16 [8192, 256], P(('row', 'col')), may hold values from -0.4 to 0.4, as said below
- spread: float32 [8192], P(('row', 'col')), may hold values from 1 to 12
- vectors: bfloat16 [8192, 64], P(('row', 'col')), may hold values from -6 to 6
Outputs:
- product: float32 [8192, 64], P(('row', 'col'))
Inputs may be any that keep to these rules, and one draw needn't show every extreme that they name: `points`: embedding entries are real values of order 0.1.
All inputs are finite; a program needn't handle non-finite values.
Results may differ from a plain program's by a relative error of at most 0.0085.
Values may be sent and summed in bfloat16 or wider, within the bound.
A program may use at most 128 MiB of HBM per device.

v0:
```python
import jax
import jax.numpy as jnp
from jax import lax
from jax.sharding import PartitionSpec as P


def distances(left_pts, right_pts):
    left_f = left_pts.astype(jnp.float32)
    right_f = right_pts.astype(jnp.float32)
    left_sq = jnp.sum(left_f * left_f, axis=1)
    right_sq = jnp.sum(right_f * right_f, axis=1)
    cross = lax.dot_general(
        left_pts, right_pts, (((1,), (1,)), ((), ())), preferred_element_type=jnp.float32
    )
    return left_sq[:, None] + right_sq[None, :] - 2.0 * cross


def local(points, spread, vectors):
    share_rows = points.shape[0]
    n_rows = lax.axis_size("row")
    n_cols = lax.axis_size("col")
    row_pos = lax.axis_index("row")
    col_pos = lax.axis_index("col")
    blk_pts, blk_bw, blk_vec = (
        lax.all_gather(points, "col", axis=0, tiled=True),
        lax.all_gather(spread.astype(jnp.bfloat16), "col", axis=0, tiled=True).astype(spread.dtype),
        lax.all_gather(vectors, "col", axis=0, tiled=True),
    )
    crs_pts, crs_bw, crs_vec = (
        lax.all_gather(points, "row", axis=0, tiled=True),
        lax.all_gather(spread.astype(jnp.bfloat16), "row", axis=0, tiled=True).astype(spread.dtype),
        lax.all_gather(vectors, "row", axis=0, tiled=True),
    )
    blk_local = jnp.arange(share_rows * n_cols, dtype=jnp.int32)
    blk_ids = row_pos * (n_cols * share_rows) + blk_local
    crs_local = jnp.arange(share_rows * n_rows, dtype=jnp.int32)
    crs_ids = (
        crs_local // share_rows * (n_cols * share_rows)
        + col_pos * share_rows
        + crs_local % share_rows
    )
    same = blk_ids[:, None] == crs_ids[None, :]
    dist = distances(blk_pts, crs_pts)
    kernel = jnp.where(same, jnp.float32(0.0), jnp.exp(-blk_bw[:, None] * dist))
    totals = lax.psum(jnp.sum(kernel, axis=1), "col")
    norm = (kernel / totals[:, None]).astype(jnp.bfloat16)
    to_cross = lax.dot_general(
        norm, blk_vec, (((0,), (0,)), ((), ())), preferred_element_type=jnp.float32
    )
    mirror = jnp.where(same, jnp.float32(0.0), jnp.exp(-crs_bw[None, :] * dist))
    mirror_tot = lax.psum(jnp.sum(mirror, axis=0), "row")
    mirror_norm = (mirror / mirror_tot[None, :]).astype(jnp.bfloat16)
    to_cross = to_cross + lax.dot_general(
        mirror_norm, blk_vec, (((0,), (0,)), ((), ())), preferred_element_type=jnp.float32
    )
    summed = lax.psum_scatter(to_cross, "row", scatter_dimension=0, tiled=True)
    return 0.5 * summed


def solution(mesh):
    placed = (P(("row", "col"), None), P(("row", "col")), P(("row", "col"), None))
    return jax.shard_map(
        local, mesh=mesh, in_specs=placed, out_specs=P(("row", "col"), None), check_vma=False
    )
```

profile of v0, /device:TPU:0, one launch (start us, length us, event | category | flops | bytes accessed | tf_op | source)
XLA Modules:
  0.0 126.9 jit_solution(6512187139585747209)
XLA Ops:
  6.5 0.0 all-gather.4.cloned.1.call-start
  6.5 0.7 all-gather.4.cloned.1.call-update
  7.3 0.0 reduce-scatter.2.cloned.1.call-start
  7.3 0.7 convert_element_type.22
  8.0 9.5 %all-gather.1 = bf16[4,1,256]{2,1,0:T(2,128)(2,1)S(1)} all-gather(bf16[1,1,256]{2,1,0:T(2,128)(2,1)S(1)} %reshape.35), channel_id=1, replica_groups=mesh['row'=4,'col'=8] {'row'}, dimensions={0}, use_global_device_ids=true | all-gather | bytes 2560 | tf_op jit(solution)/shard_map/all_gather | solution.py:31
  17.5 12.0 %all-gather = bf16[8,1,256]{2,1,0:T(2,128)(2,1)S(1)} all-gather(bf16[1,1,256]{2,1,0:T(2,128)(2,1)S(1)} %reshape.35), channel_id=1, replica_groups=mesh['row'=4,'col'=8] {'col'}, dimensions={0}, use_global_device_ids=true | all-gather | bytes 4608 | tf_op jit(solution)/shard_map/all_gather | solution.py:26
  29.5 10.3 %all_gather.17 = bf16[1024,256]{1,0:T(8,128)(2,1)S(1)} all-gather(bf16[256,256]{1,0:T(8,128)(2,1)} %param.3), channel_id=1, replica_groups=mesh['row'=4,'col'=8] {'row'}, dimensions={0}, use_global_device_ids=true | all-gather | bytes 655360 | tf_op jit(solution)/shard_map/all_gather | solution.py:30
  39.8 14.4 %all_gather.18 = bf16[2048,64]{0,1:T(8,128)(2,1)S(1)} all-gather(bf16[256,64]{0,1:T(8,128)(2,1)} %param.5), channel_id=1, replica_groups=mesh['row'=4,'col'=8] {'col'}, dimensions={0}, use_global_device_ids=true | all-gather | bytes 294912 | tf_op jit(solution)/shard_map/all_gather | solution.py:27
  54.2 0.2 multiply_reduce_fusion.1
  54.5 0.0 all-gather.4.cloned.1.call-done
  54.5 1.6 %multiply_reduce_fusion = f32[2048]{0:T(1024)S(1)} fusion(bf16[2048,256]{1,0:T(8,128)(2,1)} %all-gather.4.cloned.1.call-done), kind=kLoop, calls=%fused_computation.9 | loop fusion | flops 1570816 | bytes 1056768 | tf_op jit(solution)/shard_map/reduce_sum | solution.py:10
  56.1 7.5 %fusion = (f32[2048]{0:T(1024)S(1)}, f32[1024]{0:T(1024)S(1)}, f32[2048,1024]{1,0:T(8,128)}) fusion(f32[1024]{0:T(1024)S(1)} %multiply_reduce_fusion.1, f32[2048]{0:T(1024)S(1)} %multiply_reduce_fusion, f32[2048]{0:T(1024)S(1)} %bitcast.6, s32[1024]{0:T(1024)S(1)} %fusion.13, s32[2048]{0:T(1024)S(1)} %iota_add_fusion, f32[1024]{0:T(1024)S(1)} %bitcast.8, ...), kind=kOutput, calls=%fused_computation.5 | convolution fusion | flops 1094710272 | bytes 10010624 | tf_op jit(solution)/shard_map/dot_general | solution.py:12
  63.6 8.9 %psum.15 = f32[1024]{0:T(1024)S(1)} all-reduce(f32[1024]{0:T(1024)S(1)} %get-tuple-element.6), channel_id=1, replica_groups=mesh['row'=4,'col'=8] {'row'}, use_global_device_ids=true, to_apply=%region_5.6 | all-reduce | flops 1024 | bytes 8192 | tf_op jit(solution)/shard_map/psum | solution.py:51
  72.5 13.9 %psum.14 = f32[2048]{0:T(1024)S(1)} all-reduce(f32[2048]{0:T(1024)S(1)} %get-tuple-element.5), channel_id=1, replica_groups=mesh['row'=4,'col'=8] {'col'}, use_global_device_ids=true, to_apply=%region_3.4 | all-reduce | flops 2048 | bytes 16384 | tf_op jit(solution)/shard_map/psum | solution.py:45
  86.4 0.0 copy-start
  86.4 6.9 %fusion.2 = f32[1024,64]{0,1:T(8,128)S(1)} fusion(bf16[2048,64]{0,1:T(8,128)(2,1)S(1)} %all_gather.18, f32[2048,1024]{1,0:T(8,128)} %get-tuple-element.7, f32[1024]{0:T(1024)S(1)} %psum.15, f32[1024]{0:T(1024)S(1)} %bitcast.9, f32[1024]{0:T(1024)S(1)} %multiply_reduce_fusion.1, f32[2048]{0:T(1024)S(1)} %multiply_reduce_fusion, s32[1024]{0:T(1024)S(1)} %fusion.13, ...), kind=kOutput, calls=%fused_computation.7 | convolution fusion | flops 285212672 | bytes 8945664 | tf_op jit(solution)/shard_map/dot_general | solution.py:53
  93.3 0.0 copy-done
  93.3 3.8 %fusion.4 = f32[1024,64]{0,1:T(8,128)} fusion(f32[1024,64]{0,1:T(8,128)S(1)} %fusion.2, bf16[2048,64]{0,1:T(8,128)(2,1)S(1)} %all_gather.18, f32[2048,1024]{1,0:T(8,128)S(1)} %copy-done, f32[2048]{0:T(1024)S(1)} %psum.14, f32[1024]{0:T(1024)S(1)} %multiply_reduce_fusion.1, f32[2048]{0:T(1024)S(1)} %multiply_reduce_fusion, f32[2048]{0:T(1024)S(1)} %bitcast.7, ...), kind=kOutput, calls=%fused_computation.10 | convolution fusion | flops 285278208 | bytes 9216000 | tf_op jit(solution)/shard_map/dot_general | solution.py:47
  97.1 0.0 reduce-scatter.2.cloned.1.call-update
  97.2 21.5 %reduce-scatter.2.cloned.1.call-done = f32[256,64]{0,1:T(8,128)} async-done(((f32[1024,64]{0,1:T(8,128)}), f32[256,64]{0,1:T(8,128)}) %reduce-scatter.2.cloned.1.call-update) | async-done | bytes 65552 | tf_op jit(solution)/shard_map/reduce_scatter | solution.py:56
  118.6 1.5 %broadcast_multiply_fusion = f32[256,64]{0,1:T(8,128)} fusion(f32[256,64]{0,1:T(8,128)} %reduce-scatter.2.cloned.1.call-done), kind=kLoop, calls=%fused_computation.12 | loop fusion | flops 16384 | bytes 131072 | tf_op jit(solution)/shard_map/mul | solution.py:57
  (5 shorter events, 0.0 us)
Async XLA Ops:
  6.5 47.9 %all-gather.4.cloned.1.call-start = ((), (), s32[]{:S(2)}) async-start(), calls=%async_computation.1 | async-start | bytes 1179648 | tf_op jit(solution)/shard_map/all_gather | solution.py:25
  7.3 111.4 %reduce-scatter.2.cloned.1.call-start = ((), (), s32[]{:S(2)}) async-start(), calls=%async_computation.2 | async-start | bytes 327680 | tf_op jit(solution)/shard_map/reduce_scatter | solution.py:56
  86.4 6.9 %copy-start = (f32[2048,1024]{1,0:T(8,128)S(1)}, f32[2048,1024]{1,0:T(8,128)}, u32[]{:S(2)}) copy-start(f32[2048,1024]{1,0:T(8,128)} %get-tuple-element.7) | copy-start | bytes 25165828
Sparse Core Ops, SparseCore 0:
  9.0 24.7 all-gather.3
  97.3 21.3 reduce-scatter.1
where the time goes:
time: 127 us
  blocking collectives  69 us (54%)
  waiting for transfers between devices  22.2 us (17%)
  matrix products  18.2 us (14%)
  between operations  13.5 us (11%)
  other arithmetic  3.97 us (3%)
    reduce_scatter x1, waiting for transfers between devices, local(): summed = lax.psum_scatter(to_cross, 'row', scatter_dimension=0, tiled=True)  21.5 us
    all_gather x1, blocking collectives, local(): lax.all_gather(vectors, 'col', axis=0, tiled=True)  14.4 us
    psum x1, blocking collectives, local(): totals = lax.psum(jnp.sum(kernel, axis=1), 'col')  13.9 us
    all_gather x1, blocking collectives, local(): lax.all_gather(spread.astype(jnp.bfloat16), 'col', axis=0, tiled=True)  12 us
    all_gather x1, blocking collectives, local(): lax.all_gather(points, 'row', axis=0, tiled=True)  10.3 us
    all_gather x1, blocking collectives, local(): lax.all_gather(spread.astype(jnp.bfloat16), 'row', axis=0, tiled=True)  9.5 us
    psum x1, blocking collectives, local(): mirror_tot = lax.psum(jnp.sum(mirror, axis=0), 'row')  8.9 us
    dot_general x1, matrix products, distances(): lax.dot_general(left_pts, right_pts, (((1,), (1,)), ((), ())), preferred_...  7.5 us
  transfers between devices with their start and end apart: 2, of which 1 were waited for; matrix products, arithmetic and copies ran while one was open for 1% of the time, Pallas kernels for 0%

commit v1 on v0

v1 whole, which is shorter than its diff:
```python
import functools
import math

import jax
import jax.numpy as jnp
from jax import lax
from jax.experimental import pallas as pl
from jax.experimental.pallas import tpu as pltpu
from jax.sharding import PartitionSpec as P

MESH = pl.DeviceIdType.MESH
LOG2E = math.log2(math.e)
VMEM_SPEC = pl.BlockSpec(memory_space=pltpu.VMEM)


def fold(block):
    half = block.shape[0] // 2
    return jnp.concatenate([block[:half], block[half:]], axis=1)


def unfold(block):
    width = block.shape[1] // 2
    return jnp.concatenate([block[:, :width], block[:, width:]], axis=0)


def kernel(
    n_rows, n_cols, pts_ref, bw_ref, vec_ref, out_ref,
    blk_pts, blk_vec, blk_aux, crs_pts, crs_aux, crs_col,
    fwd_acc, mirror, part, t_in, fwd_out, fwd_in, rev_out, rev_in,
    pts_s, pts_r, vec_s, vec_r, aux_s, aux_r,
    cp_s, cp_r, ca_s, ca_r, t_s, t_r, f_s, f_r, g_s, g_r,
):
    row = lax.axis_index("row")
    col = lax.axis_index("col")
    share = pts_ref.shape[0]

    def col_peer(x):
        return {"col": lax.bitwise_xor(col, x)}

    def row_peer(x):
        return {"row": lax.bitwise_xor(row, x)}

    barrier = pltpu.get_barrier_semaphore()
    for x in range(1, n_cols):
        pl.semaphore_signal(barrier, inc=1, device_id=col_peer(x), device_id_type=MESH)
    for x in range(1, n_rows):
        pl.semaphore_signal(barrier, inc=1, device_id=row_peer(x), device_id_type=MESH)

    blk_pts[0] = pts_ref[...]
    blk_vec[0] = fold(vec_ref[...])
    pl.semaphore_wait(barrier, n_cols + n_rows - 2)

    def send(buf, src, dst, send_sem, recv_sem, peer):
        copy = pltpu.make_async_remote_copy(
            src_ref=buf.at[src], dst_ref=buf.at[dst], send_sem=send_sem.at[dst],
            recv_sem=recv_sem.at[dst], device_id=peer, device_id_type=MESH,
        )
        copy.start()
        return copy

    pts, vec, aux, cpts, caux = {}, {}, {}, {}, {}
    near = list(range(2, n_cols, 2))
    for x in near:
        pts[x] = send(blk_pts, 0, x, pts_s, pts_r, col_peer(x))
    for x in range(1, n_rows):
        copy = pltpu.make_async_remote_copy(
            src_ref=blk_pts.at[0], dst_ref=crs_pts.at[x], send_sem=cp_s.at[x],
            recv_sem=cp_r.at[x], device_id=row_peer(x), device_id_type=MESH,
        )
        copy.start()
        cpts[x] = copy
    for x in near:
        vec[x] = send(blk_vec, 0, x, vec_s, vec_r, col_peer(x))
    pts[1] = send(blk_pts, 0, 1, pts_s, pts_r, col_peer(1))
    vec[1] = send(blk_vec, 0, 1, vec_s, vec_r, col_peer(1))

    own = pts_ref[...].astype(jnp.float32)
    half_sq = 0.5 * jnp.sum(own * own, axis=1, keepdims=True)
    wide = jnp.transpose(jnp.broadcast_to(half_sq, (share, 128)))
    my_aux = jnp.concatenate([bw_ref[...] * (2.0 * LOG2E), wide[0:1]], axis=0)
    blk_aux[0] = my_aux
    crs_aux[0] = my_aux
    for x in near + [1]:
        aux[x] = send(blk_aux, 0, x, aux_s, aux_r, col_peer(x))
    for x in range(1, n_rows):
        caux[x] = send(crs_aux, 0, x, ca_s, ca_r, row_peer(x))
    crs_pts[0] = pts_ref[...]

    def column(m):
        rows = crs_aux[m]
        padded = jnp.concatenate([rows, jnp.zeros((6, share), jnp.float32)], axis=0)
        crs_col[m] = jnp.transpose(padded)

    def tile(m, b, vb, arow, hrow, diagonal):
        cols = crs_col[m]
        cross = lax.dot_general(
            crs_pts[m], blk_pts[b], (((1,), (1,)), ((), ())), preferred_element_type=jnp.float32
        )
        near_ = (cross - cols[:, 1:2]) - hrow
        first = jnp.exp2(near_ * cols[:, 0:1])
        second = jnp.exp2(near_ * arow)
        if diagonal:
            same = lax.broadcasted_iota(jnp.int32, (share, share), 0) == lax.broadcasted_iota(
                jnp.int32, (share, share), 1
            )
            first = jnp.where(same, 0.0, first)
            second = jnp.where(same, 0.0, second)
        product = jnp.dot(first.astype(jnp.bfloat16), vb, preferred_element_type=jnp.float32)
        if b == 0:
            fwd_acc[m] = product
        else:
            fwd_acc[m] += product
        mirror[m, :, b * share : (b + 1) * share] = second.astype(jnp.bfloat16)
        return jnp.sum(second, axis=0, keepdims=True)

    def step(b):
        vb = unfold(blk_vec[b])
        arow = blk_aux[b, 0:1]
        hrow = blk_aux[b, 1:2]
        if b == 0:
            column(0)
            total = tile(0, 0, vb, arow, hrow, True)
            for m in range(1, n_rows):
                cpts[m].wait_recv()
                caux[m].wait_recv()
                column(m)
                total = total + tile(m, 0, vb, arow, hrow, False)
        else:
            total = lax.fori_loop(
                0, n_rows,
                lambda m, acc: acc + tile(m, b, vb, arow, hrow, False),
                jnp.zeros((1, share), jnp.float32),
            )
        part[b : b + 1] = total

    step(0)
    for b in range(1, n_cols):
        if b % 2 == 1 and b > 1:
            pass
        pts[b].wait_recv()
        vec[b].wait_recv()
        aux[b].wait_recv()
        if b % 2 == 0:
            pts[b + 1] = send(blk_pts, b, b + 1, pts_s, pts_r, col_peer(1))
            vec[b + 1] = send(blk_vec, b, b + 1, vec_s, vec_r, col_peer(1))
            aux[b + 1] = send(blk_aux, b, b + 1, aux_s, aux_r, col_peer(1))
        step(b)

    totals = {}
    for x in range(1, n_cols):
        copy = pltpu.make_async_remote_copy(
            src_ref=part, dst_ref=t_in.at[x], send_sem=t_s.at[x], recv_sem=t_r.at[x],
            device_id=col_peer(x), device_id_type=MESH,
        )
        copy.start()
        totals[x] = copy
    fwd, rev = {}, {}
    for m in range(1, n_rows):
        fwd_out[m] = fold(fwd_acc[m]).astype(jnp.bfloat16)
        copy = pltpu.make_async_remote_copy(
            src_ref=fwd_out.at[m], dst_ref=fwd_in.at[m], send_sem=f_s.at[m], recv_sem=f_r.at[m],
            device_id=row_peer(m), device_id_type=MESH,
        )
        copy.start()
        fwd[m] = copy

    sums = [part[b : b + 1] for b in range(n_cols)]
    for x in range(1, n_cols):
        totals[x].wait_recv()
        other = t_in[x]
        for b in range(n_cols):
            sums[b] = sums[b] + other[x ^ b : (x ^ b) + 1]
    inverse = jnp.transpose(0.125 / jnp.concatenate(sums, axis=0))
    scaled = jnp.concatenate(
        [
            (unfold(blk_vec[b]).astype(jnp.float32) * inverse[:, b : b + 1]).astype(jnp.bfloat16)
            for b in range(n_cols)
        ],
        axis=0,
    )
    for m in range(1, n_rows):
        product = jnp.dot(mirror[m], scaled, preferred_element_type=jnp.float32)
        rev_out[m] = fold(product).astype(jnp.bfloat16)
        copy = pltpu.make_async_remote_copy(
            src_ref=rev_out.at[m], dst_ref=rev_in.at[m], send_sem=g_s.at[m], recv_sem=g_r.at[m],
            device_id=row_peer(m), device_id_type=MESH,
        )
        copy.start()
        rev[m] = copy
    reverse = jnp.dot(mirror[0], scaled, preferred_element_type=jnp.float32)
    forward = fwd_acc[0]
    for m in range(1, n_rows):
        fwd[m].wait_recv()
        forward = forward + unfold(fwd_in[m].astype(jnp.float32))
    for m in range(1, n_rows):
        rev[m].wait_recv()
        reverse = reverse + unfold(rev_in[m].astype(jnp.float32))
    out_ref[...] = 4.0 * (forward * inverse[:, 0:1] + reverse)
    for group in (pts, vec, aux, cpts, caux, totals, fwd, rev):
        for copy in group.values():
            copy.wait_send()


def local(n_rows, n_cols, points, spread, vectors):
    share, width = points.shape
    k = vectors.shape[1]
    f32, bf16 = jnp.float32, jnp.bfloat16
    dma = pltpu.SemaphoreType.DMA
    scratch = [
        pltpu.VMEM((n_cols, share, width), bf16),
        pltpu.VMEM((n_cols, share // 2, 2 * k), bf16),
        pltpu.VMEM((n_cols, 2, share), f32),
        pltpu.VMEM((n_rows, share, width), bf16),
        pltpu.VMEM((n_rows, 2, share), f32),
        pltpu.VMEM((n_rows, share, 8), f32),
        pltpu.VMEM((n_rows, share, k), f32),
        pltpu.VMEM((n_rows, share, n_cols * share), bf16),
        pltpu.VMEM((n_cols, share), f32),
        pltpu.VMEM((n_cols, n_cols, share), f32),
    ] + [pltpu.VMEM((n_rows, share // 2, 2 * k), bf16)] * 4
    scratch += [dma((n_cols,))] * 6 + [dma((n_rows,))] * 4 + [dma((n_cols,))] * 2
    scratch += [dma((n_rows,))] * 4
    return pl.pallas_call(
        functools.partial(kernel, n_rows, n_cols),
        out_shape=jax.ShapeDtypeStruct((share, k), f32),
        in_specs=[VMEM_SPEC] * 3,
        out_specs=VMEM_SPEC,
        scratch_shapes=scratch,
        compiler_params=pltpu.CompilerParams(
            collective_id=0, has_side_effects=True, vmem_limit_bytes=56 * 1024 * 1024
        ),
    )(points, spread.reshape(1, share), vectors)


def solution(mesh):
    placed = (P(("row", "col"), None), P(("row", "col")), P(("row", "col"), None))
    return jax.shard_map(
        functools.partial(local, mesh.shape["row"], mesh.shape["col"]),
        mesh=mesh, in_specs=placed, out_specs=P(("row", "col"), None), check_vma=False,
    )
```

time: 127 us -> 43.9 us (0.35)
  blocking collectives: 69 us -> 0 us
  Pallas kernels: 0 us -> 40.6 us
  waiting for transfers between devices: 22.2 us -> 0 us
  matrix products: 18.2 us -> 0 us
  between operations: 13.5 us -> 0.01 us
  other arithmetic: 3.97 us -> 0 us
  local copies, waits for them, and re-layouts: 0.01 us -> 3.11 us
    all_gather x4 -> x0, blocking collectives: 46.2 us -> none  [the longest x1 14.4 us: local(): lax.all_gather(vectors, 'col', axis=0, tiled=True)]
    pallas_call x0 -> x1, Pallas kernels: none -> 40.6 us  [local(): pl.pallas_call(functools.partial(kernel, n_rows, n_cols), out_shape=jax.S...]
    psum x2 -> x0, blocking collectives: 22.8 us -> none  [the longest x1 13.9 us: local(): totals = lax.psum(jnp.sum(kernel, axis=1), 'col')]
    reduce_scatter x1 -> x0, waiting for transfers between devices: 21.5 us -> none  [local(): summed = lax.psum_scatter(to_cross, 'row', scatter_dimension=0, tiled=True)]
    dot_general x3 -> x0, matrix products: 18.2 us -> none  [the longest x1 7.5 us: distances(): lax.dot_general(left_pts, right_pts, (((1,), (1,)), ((), ())), preferred_...]
    reduce_sum x2 -> x0, other arithmetic: 1.78 us -> none  [the longest x1 1.57 us: distances(): left_sq = jnp.sum(left_f * left_f, axis=1)]
    pallas_call x0 -> x1, local copies, waits for them, and re-layouts: none -> 1.62 us  [local(): pl.pallas_call(functools.partial(kernel, n_rows, n_cols), out_shape=jax.S...]
    unnamed x3 -> x1, local copies, waits for them, and re-layouts: 0.01 us -> 1.49 us
  transfers between devices with their start and end apart: 2 -> 0, of which waited for: 1 -> 0; matrix products, arithmetic and copies ran while one was open for 1% -> 0% of each run, Pallas kernels for 0% -> 0%
where the time goes in v1:
time: 43.9 us; the launch traced here: 43.7 us
  Pallas kernels  40.6 us (92%)
  local copies, waits for them, and re-layouts  3.11 us (7%)
    pallas_call x1, Pallas kernels, local(): pl.pallas_call(functools.partial(kernel, n_rows, n_cols), out_shape=jax.S...  40.6 us
    pallas_call x1, local copies, waits for them, and re-layouts, local(): pl.pallas_call(functools.partial(kernel, n_rows, n_cols), out_shape=jax.S...  1.62 us
    unnamed x1, local copies, waits for them, and re-layouts  1.49 us

profile of v1, /device:TPU:0, one launch (start us, length us, event | category | flops | bytes accessed | tf_op | source)
XLA Modules:
  0.0 43.7 jit_solution(1076822832751253629)
XLA Ops:
  0.0 1.5 %copy.4.vec_ref = bf16[256,64]{1,0:T(8,128)(2,1)} copy(bf16[256,64]{0,1:T(8,128)(2,1)} %param.5) | data formatting | bytes 65536 | tf_op args[2]
  1.5 40.6 %shard_map.37 = f32[256,64]{1,0:T(8,128)} custom-call(bf16[256,256]{1,0:T(8,128)(2,1)} %pts_ref.1, f32[1,256]{1,0:T(1,128)} %bitcast.1, bf16[256,64]{1,0:T(8,128)(2,1)} %copy.4.vec_ref), custom_call_target="tpu_custom_call" | custom-call | tf_op jit(solution)/shard_map/pallas_call | solution.py:223
  42.1 1.6 %copy.5 = f32[256,64]{0,1:T(8,128)} copy(f32[256,64]{1,0:T(8,128)} %shard_map.37) | data formatting | bytes 131072 | tf_op jit(solution)/shard_map/pallas_call | solution.py:223

commit v2 on v0

v2 whole, which is shorter than its diff:
```python
import functools
import math

import jax
import jax.numpy as jnp
from jax import lax
from jax.experimental import pallas as pl
from jax.experimental.pallas import tpu as pltpu
from jax.sharding import PartitionSpec as P

MESH = pl.DeviceIdType.MESH
LOG2E = math.log2(math.e)
VMEM_SPEC = pl.BlockSpec(memory_space=pltpu.VMEM)
HEAD = 16
NT = (((1,), (1,)), ((), ()))


def terms(value):
    high = value.astype(jnp.bfloat16)
    rest = value - high.astype(jnp.float32)
    middle = rest.astype(jnp.bfloat16)
    return [high, middle, (rest - middle.astype(jnp.float32)).astype(jnp.bfloat16)]


def untangle(head):
    head = head.astype(jnp.float32)
    return head[0:1] + head[1:2] + head[2:3], head[3:4] + head[4:5] + head[5:6]


def kernel(
    n_rows, n_cols, pts_ref, bw_ref, vec_ref, out_ref,
    blk, crs, crs_col, direct, mirror, vec_all, part, t_in, inv,
    fwd_out, fwd_in, rev_out, rev_in,
    zs, zr, ss, sr, cs, cr, ts, tr, fs, fr, gs, gr,
):
    share, width = pts_ref.shape
    k_vec = vec_ref.shape[0]
    f32, bf16 = jnp.float32, jnp.bfloat16
    n = n_cols // 2
    half = HEAD + share // 2
    chunks = [(0, half), (half, share // 2), (HEAD + share, k_vec)]
    row = lax.axis_index("row")
    col = lax.axis_index("col")
    p = col // 2
    core = col % 2
    square = n_rows == 4
    sibling = {"col": p * 2 + 1 - core}

    def row_peer(m):
        return {"row": lax.bitwise_xor(row, m)}

    near_rows = [1, 2] if square else list(range(1, n_rows))
    barrier = pltpu.get_barrier_semaphore()
    pl.semaphore_signal(barrier, inc=1, device_id=sibling, device_id_type=MESH)
    for m in near_rows:
        pl.semaphore_signal(barrier, inc=1, device_id=row_peer(m), device_id_type=MESH)
    has_left = p > 0
    has_right = p < n - 1

    @pl.when(has_left)
    def _():
        pl.semaphore_signal(barrier, inc=1, device_id={"col": col - 2}, device_id_type=MESH)

    @pl.when(has_right)
    def _():
        pl.semaphore_signal(barrier, inc=1, device_id={"col": col + 2}, device_id_type=MESH)

    own = pts_ref[...].astype(f32)
    half_sq = 0.5 * jnp.sum(own * own, axis=1, keepdims=True)
    wide = jnp.transpose(jnp.broadcast_to(half_sq, (share, 128)))
    head = jnp.concatenate(
        [t.astype(f32) for t in terms(bw_ref[...] * (2.0 * LOG2E)) + terms(wide[0:1])]
        + [jnp.zeros((HEAD - 6, share), f32)],
        axis=0,
    ).astype(bf16)
    blk[col, 0:HEAD] = head
    blk[col, HEAD : HEAD + share] = pts_ref[...]
    blk[col, HEAD + share :] = vec_ref[...]
    crs[0, 0:HEAD] = head
    crs[0, HEAD:] = pts_ref[...]
    part[...] = jnp.zeros_like(part)

    beside = has_left.astype(jnp.int32) + has_right.astype(jnp.int32)
    pl.semaphore_wait(barrier, beside + (1 + len(near_rows)))

    def rows(c):
        return pl.ds(chunks[c][0], chunks[c][1])

    def z_copy(side, k, c):
        slot = col + (2 * k if side else -2 * k)
        return pltpu.make_async_remote_copy(
            src_ref=blk.at[slot, rows(c)], dst_ref=blk.at[slot, rows(c)],
            send_sem=zs.at[side, k, c], recv_sem=zr.at[side, k + 1, c],
            device_id={"col": col - 2 if side else col + 2}, device_id_type=MESH,
        )

    def sib_copy(side, k, c, slot):
        return pltpu.make_async_remote_copy(
            src_ref=blk.at[slot, rows(c)], dst_ref=blk.at[slot, rows(c)],
            send_sem=ss.at[side, k, c], recv_sem=sr.at[side, k, c],
            device_id=sibling, device_id_type=MESH,
        )

    def comes(side, k):
        return p + k <= n - 1 if side else p - k >= 0

    def leaves(side, k):
        return comes(side, k) & (has_left if side else has_right)

    def z_send(k, c):
        for side in (0, 1):
            pl.when(leaves(side, k))(lambda: z_copy(side, k, c).start())

    def slot_at(side, k):
        return col + (2 * k if side else -2 * k)

    def z_arrive(k, c):
        for side in (0, 1):

            @pl.when(comes(side, k))
            def _():
                slot = slot_at(side, k)
                pltpu.make_async_remote_copy(
                    src_ref=blk.at[slot, rows(c)], dst_ref=blk.at[slot, rows(c)],
                    send_sem=zs.at[side, k, c], recv_sem=zr.at[side, k, c],
                    device_id=sibling, device_id_type=MESH,
                ).wait_recv()

            if k < n - 1:
                pl.when(leaves(side, k))(lambda: z_copy(side, k, c).start())
            pl.when(comes(side, k))(lambda: sib_copy(side, k, c, slot_at(side, k)).start())

    def sib_arrive(k, cs_):
        other = p * 2 + 1 - core
        for side in (0, 1):
            if k == 0 and side:
                continue

            @pl.when(comes(side, k))
            def _():
                for c in cs_:
                    sib_copy(side, k, c, other + (2 * k if side else -2 * k)).wait_recv()

    def c_copy(src, dst, c, peer):
        source = blk.at[col, rows(c)] if src == 0 else crs.at[src, rows(c)]
        return pltpu.make_async_remote_copy(
            src_ref=source, dst_ref=crs.at[dst, rows(c)],
            send_sem=cs.at[dst, c], recv_sem=cr.at[dst, c], device_id=peer, device_id_type=MESH,
        )

    cross_copies = {}

    def c_send(src, dst, c, peer):
        cross_copies[dst, c] = c_copy(src, dst, c, peer)
        cross_copies[dst, c].start()

    for c in (0, 1):
        z_send(0, c)
        for m in near_rows:
            c_send(0, m, c, row_peer(m))
    for c in (0, 1, 2):
        sib_copy(0, 0, c, col).start()
    z_send(0, 2)

    def column(m):
        spread_row, half_row = untangle(crs[m, 0:HEAD])
        padded = jnp.concatenate([spread_row, half_row, jnp.zeros((6, share), f32)], axis=0)
        crs_col[m] = jnp.transpose(padded)

    def tile(m, slot, diagonal=False):
        cols = crs_col[m]
        arow, hrow = untangle(blk[slot, 0:HEAD])
        cross = lax.dot_general(
            crs[m, HEAD:], blk[slot, HEAD : HEAD + share], NT, preferred_element_type=f32
        )
        near = (cross - cols[:, 1:2]) - hrow
        first = jnp.exp2(near * cols[:, 0:1])
        second = jnp.exp2(near * arow)
        if diagonal:
            same = lax.broadcasted_iota(jnp.int32, (share, share), 0) == lax.broadcasted_iota(
                jnp.int32, (share, share), 1
            )
            first = jnp.where(same, 0.0, first)
            second = jnp.where(same, 0.0, second)
        where = pl.ds(pl.multiple_of(slot * share, share), share)
        direct[m, :, where] = first.astype(bf16)
        mirror[m, :, where] = second.astype(bf16)
        part[slot] += jnp.sum(second, axis=0, keepdims=True)

    def tiles(q, first_m, last_m):
        count = last_m - first_m

        def body(index, carry):
            tile(first_m + index % count, q * 2 + index // count)
            return carry

        if count > 0:
            lax.fori_loop(0, 2 * count, body, 0)

    def nth(s):
        both = jnp.minimum(p, n - 1 - p)
        k_one = s // 2 + 1
        k_two = s - both + 1
        early = p - k_one if s % 2 == 0 else p + k_one
        late = jnp.where(2 * p < n - 1, p + k_two, p - k_two)
        return jnp.where(s < 2 * both, early, late)

    column(0)
    tile(0, col, True)
    sib_arrive(0, (0, 1))
    tile(0, p * 2 + 1 - core)
    for c in (0, 1):
        z_arrive(1, c)
        for m in near_rows:
            cross_copies[m, c].wait_recv()
        if square:
            c_send(*((1, 3, 0, row_peer(2)) if c == 0 else (2, 3, 1, row_peer(1))))
    last = near_rows[-1] + 1
    for m in near_rows:
        column(m)
    tiles(p, 1, last)

    def compute(s, stop):
        sib_arrive(s + 1, (0, 1))
        tiles(nth(s), 0, stop)

    if n > 2:
        z_arrive(2, 0)
        z_arrive(2, 1)
    compute(0, last)
    if square:
        cross_copies[3, 0].wait_recv()
        cross_copies[3, 1].wait_recv()
        column(3)
        tiles(p, 3, 4)
        tiles(nth(0), 3, 4)
    z_arrive(1, 2)
    for s in range(1, n - 1):
        if 3 <= s + 1:
            z_arrive(s + 1, 0)
            z_arrive(s + 1, 1)
        compute(s, n_rows)
        if s + 1 < n - 1:
            z_arrive(s + 1, 2)

    totals = []
    for x in range(1, n_cols):
        copy = pltpu.make_async_remote_copy(
            src_ref=part, dst_ref=t_in.at[x], send_sem=ts.at[x], recv_sem=tr.at[x],
            device_id={"col": lax.bitwise_xor(col, x)}, device_id_type=MESH,
        )
        copy.start()
        totals.append(copy)
    if n > 2:
        z_arrive(n - 1, 2)
    for k in range(n):
        sib_arrive(k, (2,))
    for q in range(n_cols):
        vec_all[:, q * share : (q + 1) * share] = blk[q, HEAD + share :]

    def reduce_send(m, value, out, in_, send, recv):
        out[m] = value.astype(bf16)
        copy = pltpu.make_async_remote_copy(
            src_ref=out.at[m], dst_ref=in_.at[m], send_sem=send.at[m], recv_sem=recv.at[m],
            device_id=row_peer(m), device_id_type=MESH,
        )
        copy.start()
        return copy

    def product(left, right):
        return lax.dot_general(left, right, NT, preferred_element_type=f32)

    order = list(range(n_rows - 1, 0, -1))
    fwd = {m: reduce_send(m, product(vec_all[...], direct[m]), fwd_out, fwd_in, fs, fr) for m in order}
    forward = product(vec_all[...], direct[0])

    total = part[...]
    for x in range(1, n_cols):
        totals[x - 1].wait_recv()
        total = total + t_in[x]
    inverse = 0.125 / total
    inv[...] = inverse
    scaled = jnp.concatenate(
        [
            (vec_all[:, q * share : (q + 1) * share].astype(f32) * inverse[q]).astype(bf16)
            for q in range(n_cols)
        ],
        axis=1,
    )
    rev = {m: reduce_send(m, product(scaled, mirror[m]), rev_out, rev_in, gs, gr) for m in order}
    reverse = product(scaled, mirror[0])
    for m in near_rows + ([3] if square else []):
        fwd[m].wait_recv()
        forward = forward + fwd_in[m].astype(f32)
    forward = forward * inv[col]
    for m in near_rows + ([3] if square else []):
        rev[m].wait_recv()
        reverse = reverse + rev_in[m].astype(f32)
    out_ref[...] = 4.0 * (forward + reverse)

    for group in (cross_copies, fwd, rev):
        for copy in group.values():
            copy.wait_send()
    for copy in totals:
        copy.wait_send()
    for c in (0, 1, 2):
        sib_copy(0, 0, c, col).wait_send()
        for side in (0, 1):
            for k in range(n):
                if k < n - 1:
                    pl.when(leaves(side, k))(lambda: z_copy(side, k, c).wait_send())
                if k > 0:
                    pl.when(comes(side, k))(
                        lambda: sib_copy(side, k, c, slot_at(side, k)).wait_send()
                    )


def local(n_rows, n_cols, points, spread, vectors):
    share, width = points.shape
    k = vectors.shape[1]
    f32, bf16 = jnp.float32, jnp.bfloat16
    dma = pltpu.SemaphoreType.DMA
    n = n_cols // 2
    scratch = [
        pltpu.VMEM((n_cols, HEAD + share + k, width), bf16),
        pltpu.VMEM((n_rows, HEAD + share, width), bf16),
        pltpu.VMEM((n_rows, share, 8), f32),
        pltpu.VMEM((n_rows, share, n_cols * share), bf16),
        pltpu.VMEM((n_rows, share, n_cols * share), bf16),
        pltpu.VMEM((k, n_cols * share), bf16),
        pltpu.VMEM((n_cols, 1, share), f32),
        pltpu.VMEM((n_cols, n_cols, 1, share), f32),
        pltpu.VMEM((n_cols, 1, share), f32),
    ] + [pltpu.VMEM((n_rows, k, share), bf16)] * 4
    scratch += [dma((2, n, 3))] * 4 + [dma((n_rows, 2))] * 2 + [dma((n_cols,))] * 2
    scratch += [dma((n_rows,))] * 4
    out = pl.pallas_call(
        functools.partial(kernel, n_rows, n_cols),
        out_shape=jax.ShapeDtypeStruct((k, share), f32),
        in_specs=[VMEM_SPEC] * 3,
        out_specs=VMEM_SPEC,
        scratch_shapes=scratch,
        compiler_params=pltpu.CompilerParams(
            collective_id=0, has_side_effects=True, vmem_limit_bytes=58 * 1024 * 1024
        ),
    )(points, spread.reshape(1, share), vectors.T)
    return out.T


def solution(mesh):
    placed = (P(("row", "col"), None), P(("row", "col")), P(("row", "col"), None))
    return jax.shard_map(
        functools.partial(local, mesh.shape["row"], mesh.shape["col"]),
        mesh=mesh, in_specs=placed, out_specs=P(("row", "col"), None), check_vma=False,
    )
```

time: 127 us -> 36.6 us (0.29)
  blocking collectives: 69 us -> 0 us
  Pallas kernels: 0 us -> 34.9 us
  waiting for transfers between devices: 22.2 us -> 0 us
  matrix products: 18.2 us -> 0 us
  between operations: 13.5 us -> 0.01 us
  other arithmetic: 3.97 us -> 0 us
  local copies, waits for them, and re-layouts: 0.01 us -> 1.47 us
    all_gather x4 -> x0, blocking collectives: 46.2 us -> none  [the longest x1 14.4 us: local(): lax.all_gather(vectors, 'col', axis=0, tiled=True)]
    pallas_call x0 -> x1, Pallas kernels: none -> 34.9 us  [local(): pl.pallas_call(functools.partial(kernel, n_rows, n_cols), out_shape=jax.S...]
    psum x2 -> x0, blocking collectives: 22.8 us -> none  [the longest x1 13.9 us: local(): totals = lax.psum(jnp.sum(kernel, axis=1), 'col')]
    reduce_scatter x1 -> x0, waiting for transfers between devices: 21.5 us -> none  [local(): summed = lax.psum_scatter(to_cross, 'row', scatter_dimension=0, tiled=True)]
    dot_general x3 -> x0, matrix products: 18.2 us -> none  [the longest x1 7.5 us: distances(): lax.dot_general(left_pts, right_pts, (((1,), (1,)), ((), ())), preferred_...]
    reduce_sum x2 -> x0, other arithmetic: 1.78 us -> none  [the longest x1 1.57 us: distances(): left_sq = jnp.sum(left_f * left_f, axis=1)]
    mul x1 -> x0, other arithmetic: 1.47 us -> none  [local(): return 0.5 * summed]
    unnamed x3 -> x1, local copies, waits for them, and re-layouts: 0.01 us -> 1.47 us
  transfers between devices with their start and end apart: 2 -> 0, of which waited for: 1 -> 0; matrix products, arithmetic and copies ran while one was open for 1% -> 0% of each run, Pallas kernels for 0% -> 0%
where the time goes in v2:
time: 36.6 us; the launch traced here: 36.4 us
  Pallas kernels  34.9 us (95%)
  local copies, waits for them, and re-layouts  1.47 us (4%)
    pallas_call x1, Pallas kernels, local(): pl.pallas_call(functools.partial(kernel, n_rows, n_cols), out_shape=jax.S...  34.9 us
    unnamed x1, local copies, waits for them, and re-layouts  1.47 us

profile of v2, /device:TPU:0, one launch (start us, length us, event | category | flops | bytes accessed | tf_op | source)
XLA Modules:
  0.0 36.4 jit_solution(15700736242204436439)
XLA Ops:
  0.0 34.9 %shard_map.37 = f32[64,256]{1,0:T(8,128)} custom-call(bf16[256,256]{1,0:T(8,128)(2,1)} %pts_ref.1, f32[1,256]{1,0:T(1,128)} %bitcast.5, bf16[64,256]{1,0:T(8,128)(2,1)} %bitcast.4), custom_call_target="tpu_custom_call" | custom-call | tf_op jit(solution)/shard_map/pallas_call | solution.py:337
  34.9 1.5 %copy.5 = f32[256,64]{0,1:T(8,128)} copy(f32[256,64]{0,1:T(8,128)} %bitcast.3) | data formatting | bytes 131072

commit v3 on v2

--- a/solution.py
+++ b/solution.py
@@ -129,6 +129,28 @@
             if k < n - 1:
                 pl.when(leaves(side, k))(lambda: z_copy(side, k, c).start())
             pl.when(comes(side, k))(lambda: sib_copy(side, k, c, slot_at(side, k)).start())
+            if c == 0:
+                pl.when(comes(side, k))(lambda: vec_copy(side, k).start())
+
+    def vec_copy(side, k):
+        return pltpu.make_async_remote_copy(
+            src_ref=blk.at[col, rows(2)], dst_ref=blk.at[col, rows(2)],
+            send_sem=zs.at[side, k, 2], recv_sem=zr.at[1 - side, k, 2],
+            device_id={"col": slot_at(side, k)}, device_id_type=MESH,
+        )
+
+    def vec_arrive(k):
+        for side in (0, 1):
+
+            @pl.when(comes(side, k))
+            def _():
+                slot = slot_at(side, k)
+                pltpu.make_async_remote_copy(
+                    src_ref=blk.at[slot, rows(2)], dst_ref=blk.at[slot, rows(2)],
+                    send_sem=zs.at[side, k, 2], recv_sem=zr.at[side, k, 2],
+                    device_id=sibling, device_id_type=MESH,
+                ).wait_recv()
+                sib_copy(side, k, 2, slot).start()
 
     def sib_arrive(k, cs_):
         other = p * 2 + 1 - core
@@ -160,7 +182,6 @@
             c_send(0, m, c, row_peer(m))
     for c in (0, 1, 2):
         sib_copy(0, 0, c, col).start()
-    z_send(0, 2)
 
     def column(m):
         spread_row, half_row = untangle(crs[m, 0:HEAD])
@@ -195,7 +216,7 @@
             return carry
 
         if count > 0:
-            lax.fori_loop(0, 2 * count, body, 0)
+            lax.fori_loop(0, 2 * count, body, 0, unroll=min(2 * count, 8))
 
     def nth(s):
         both = jnp.minimum(p, n - 1 - p)
@@ -234,14 +255,11 @@
         column(3)
         tiles(p, 3, 4)
         tiles(nth(0), 3, 4)
-    z_arrive(1, 2)
     for s in range(1, n - 1):
-        if 3 <= s + 1:
+        if s > 1:
             z_arrive(s + 1, 0)
             z_arrive(s + 1, 1)
         compute(s, n_rows)
-        if s + 1 < n - 1:
-            z_arrive(s + 1, 2)
 
     totals = []
     for x in range(1, n_cols):
@@ -251,8 +269,8 @@
         )
         copy.start()
         totals.append(copy)
-    if n > 2:
-        z_arrive(n - 1, 2)
+    for k in range(1, n):
+        vec_arrive(k)
     for k in range(n):
         sib_arrive(k, (2,))
     for q in range(n_cols):
@@ -307,8 +325,10 @@
         sib_copy(0, 0, c, col).wait_send()
         for side in (0, 1):
             for k in range(n):
-                if k < n - 1:
+                if c < 2 and k < n - 1:
                     pl.when(leaves(side, k))(lambda: z_copy(side, k, c).wait_send())
+                if c == 2 and k > 0:
+                    pl.when(comes(side, k))(lambda: vec_copy(side, k).wait_send())
                 if k > 0:
                     pl.when(comes(side, k))(
                         lambda: sib_copy(side, k, c, slot_at(side, k)).wait_send()

time: 36.6 us -> 33.1 us (0.904)
  Pallas kernels: 34.9 us -> 31.5 us
    pallas_call x1, Pallas kernels: 34.9 us -> 31.5 us  [local(): pl.pallas_call(functools.partial(kernel, n_rows, n_cols), out_shape=jax.S...]
where the time goes in v3:
time: 33.1 us; the launch traced here: 32.9 us
  Pallas kernels  31.5 us (95%)
  local copies, waits for them, and re-layouts  1.47 us (4%)
    pallas_call x1, Pallas kernels, local(): pl.pallas_call(functools.partial(kernel, n_rows, n_cols), out_shape=jax.S...  31.5 us
    unnamed x1, local copies, waits for them, and re-layouts  1.47 us

profile of v3, /device:TPU:0, one launch (start us, length us, event | category | flops | bytes accessed | tf_op | source)
XLA Modules:
  0.0 32.9 jit_solution(1912736268451457747)
XLA Ops:
  0.0 31.5 %shard_map.37 = f32[64,256]{1,0:T(8,128)} custom-call(bf16[256,256]{1,0:T(8,128)(2,1)} %pts_ref.1, f32[1,256]{1,0:T(1,128)} %bitcast.5, bf16[64,256]{1,0:T(8,128)(2,1)} %bitcast.4), custom_call_target="tpu_custom_call" | custom-call | tf_op jit(solution)/shard_map/pallas_call | solution.py:357
  31.5 1.5 %copy.5 = f32[256,64]{0,1:T(8,128)} copy(f32[256,64]{0,1:T(8,128)} %bitcast.3) | data formatting | bytes 131072

commit v4 on v3

--- a/solution.py
+++ b/solution.py
@@ -11,6 +11,8 @@
 MESH = pl.DeviceIdType.MESH
 LOG2E = math.log2(math.e)
 VMEM_SPEC = pl.BlockSpec(memory_space=pltpu.VMEM)
+ANY_SPEC = pl.BlockSpec(memory_space=pl.ANY)
+PIECES = 2
 HEAD = 16
 NT = (((1,), (1,)), ((), ()))
 
@@ -31,14 +33,18 @@
     n_rows, n_cols, pts_ref, bw_ref, vec_ref, out_ref,
     blk, crs, crs_col, direct, mirror, vec_all, part, t_in, inv,
     fwd_out, fwd_in, rev_out, rev_in,
-    zs, zr, ss, sr, cs, cr, ts, tr, fs, fr, gs, gr,
+    zs, zr, ss, sr, cs, cr, ts, tr, fs, fr, gs, gr, ls,
 ):
     share, width = pts_ref.shape
     k_vec = vec_ref.shape[0]
     f32, bf16 = jnp.float32, jnp.bfloat16
     n = n_cols // 2
     half = HEAD + share // 2
-    chunks = [(0, half), (half, share // 2), (HEAD + share, k_vec)]
+    halves = [(0, half), (half, share // 2)]
+    piece = share // PIECES
+    chunks = [(0, HEAD + piece)] + [(HEAD + c * piece, piece) for c in range(1, PIECES)]
+    chunks.append((HEAD + share, k_vec))
+    points, vecs = tuple(range(PIECES)), PIECES
     row = lax.axis_index("row")
     col = lax.axis_index("col")
     p = col // 2
@@ -65,7 +71,15 @@
     def _():
         pl.semaphore_signal(barrier, inc=1, device_id={"col": col + 2}, device_id_type=MESH)
 
-    own = pts_ref[...].astype(f32)
+    loads = [
+        pltpu.make_async_copy(pts_ref, crs.at[0, pl.ds(HEAD, share)], ls.at[0]),
+        pltpu.make_async_copy(pts_ref, blk.at[col, pl.ds(HEAD, share)], ls.at[1]),
+        pltpu.make_async_copy(vec_ref, blk.at[col, pl.ds(HEAD + share, k_vec)], ls.at[2]),
+    ]
+    for load in loads:
+        load.start()
+    loads[0].wait()
+    own = crs[0, HEAD:].astype(f32)
     half_sq = 0.5 * jnp.sum(own * own, axis=1, keepdims=True)
     wide = jnp.transpose(jnp.broadcast_to(half_sq, (share, 128)))
     head = jnp.concatenate(
@@ -74,11 +88,10 @@
         axis=0,
     ).astype(bf16)
     blk[col, 0:HEAD] = head
-    blk[col, HEAD : HEAD + share] = pts_ref[...]
-    blk[col, HEAD + share :] = vec_ref[...]
     crs[0, 0:HEAD] = head
-    crs[0, HEAD:] = pts_ref[...]
     part[...] = jnp.zeros_like(part)
+    loads[1].wait()
+    loads[2].wait()
 
     beside = has_left.astype(jnp.int32) + has_right.astype(jnp.int32)
     pl.semaphore_wait(barrier, beside + (1 + len(near_rows)))
@@ -129,13 +142,13 @@
             if k < n - 1:
                 pl.when(leaves(side, k))(lambda: z_copy(side, k, c).start())
             pl.when(comes(side, k))(lambda: sib_copy(side, k, c, slot_at(side, k)).start())
-            if c == 0:
+            if c == 0 and k > 2:
                 pl.when(comes(side, k))(lambda: vec_copy(side, k).start())
 
     def vec_copy(side, k):
         return pltpu.make_async_remote_copy(
-            src_ref=blk.at[col, rows(2)], dst_ref=blk.at[col, rows(2)],
-            send_sem=zs.at[side, k, 2], recv_sem=zr.at[1 - side, k, 2],
+            src_ref=blk.at[col, rows(vecs)], dst_ref=blk.at[col, rows(vecs)],
+            send_sem=zs.at[side, k, vecs], recv_sem=zr.at[1 - side, k, vecs],
             device_id={"col": slot_at(side, k)}, device_id_type=MESH,
         )
 
@@ -146,11 +159,11 @@
             def _():
                 slot = slot_at(side, k)
                 pltpu.make_async_remote_copy(
-                    src_ref=blk.at[slot, rows(2)], dst_ref=blk.at[slot, rows(2)],
-                    send_sem=zs.at[side, k, 2], recv_sem=zr.at[side, k, 2],
+                    src_ref=blk.at[slot, rows(vecs)], dst_ref=blk.at[slot, rows(vecs)],
+                    send_sem=zs.at[side, k, vecs], recv_sem=zr.at[side, k, vecs],
                     device_id=sibling, device_id_type=MESH,
                 ).wait_recv()
-                sib_copy(side, k, 2, slot).start()
+                sib_copy(side, k, vecs, slot).start()
 
     def sib_arrive(k, cs_):
         other = p * 2 + 1 - core
@@ -164,9 +177,10 @@
                     sib_copy(side, k, c, other + (2 * k if side else -2 * k)).wait_recv()
 
     def c_copy(src, dst, c, peer):
-        source = blk.at[col, rows(c)] if src == 0 else crs.at[src, rows(c)]
+        part_rows = pl.ds(*halves[c])
+        source = blk.at[col, part_rows] if src == 0 else crs.at[src, part_rows]
         return pltpu.make_async_remote_copy(
-            src_ref=source, dst_ref=crs.at[dst, rows(c)],
+            src_ref=source, dst_ref=crs.at[dst, part_rows],
             send_sem=cs.at[dst, c], recv_sem=cr.at[dst, c], device_id=peer, device_id_type=MESH,
         )
 
@@ -176,11 +190,12 @@
         cross_copies[dst, c] = c_copy(src, dst, c, peer)
         cross_copies[dst, c].start()
 
+    for c in points:
+        z_send(0, c)
     for c in (0, 1):
-        z_send(0, c)
         for m in near_rows:
             c_send(0, m, c, row_peer(m))
-    for c in (0, 1, 2):
+    for c in range(PIECES + 1):
         sib_copy(0, 0, c, col).start()
 
     def column(m):
@@ -228,10 +243,11 @@
 
     column(0)
     tile(0, col, True)
-    sib_arrive(0, (0, 1))
+    sib_arrive(0, points)
     tile(0, p * 2 + 1 - core)
+    for c in points:
+        z_arrive(1, c)
     for c in (0, 1):
-        z_arrive(1, c)
         for m in near_rows:
             cross_copies[m, c].wait_recv()
         if square:
@@ -242,12 +258,15 @@
     tiles(p, 1, last)
 
     def compute(s, stop):
-        sib_arrive(s + 1, (0, 1))
+        sib_arrive(s + 1, points)
         tiles(nth(s), 0, stop)
 
     if n > 2:
-        z_arrive(2, 0)
-        z_arrive(2, 1)
+        for c in points:
+            z_arrive(2, c)
+    for k in range(1, min(n, 3)):
+        for side in (0, 1):
+            pl.when(comes(side, k))(lambda: vec_copy(side, k).start())
     compute(0, last)
     if square:
         cross_copies[3, 0].wait_recv()
@@ -257,8 +276,8 @@
         tiles(nth(0), 3, 4)
     for s in range(1, n - 1):
         if s > 1:
-            z_arrive(s + 1, 0)
-            z_arrive(s + 1, 1)
+            for c in points:
+                z_arrive(s + 1, c)
         compute(s, n_rows)
 
     totals = []
@@ -272,7 +291,7 @@
     for k in range(1, n):
         vec_arrive(k)
     for k in range(n):
-        sib_arrive(k, (2,))
+        sib_arrive(k, (vecs,))
     for q in range(n_cols):
         vec_all[:, q * share : (q + 1) * share] = blk[q, HEAD + share :]
 
@@ -321,13 +340,13 @@
             copy.wait_send()
     for copy in totals:
         copy.wait_send()
-    for c in (0, 1, 2):
+    for c in range(PIECES + 1):
         sib_copy(0, 0, c, col).wait_send()
         for side in (0, 1):
             for k in range(n):
-                if c < 2 and k < n - 1:
+                if c < vecs and k < n - 1:
                     pl.when(leaves(side, k))(lambda: z_copy(side, k, c).wait_send())
-                if c == 2 and k > 0:
+                if c == vecs and k > 0:
                     pl.when(comes(side, k))(lambda: vec_copy(side, k).wait_send())
                 if k > 0:
                     pl.when(comes(side, k))(
@@ -352,12 +371,12 @@
         pltpu.VMEM((n_cols, n_cols, 1, share), f32),
         pltpu.VMEM((n_cols, 1, share), f32),
     ] + [pltpu.VMEM((n_rows, k, share), bf16)] * 4
-    scratch += [dma((2, n, 3))] * 4 + [dma((n_rows, 2))] * 2 + [dma((n_cols,))] * 2
-    scratch += [dma((n_rows,))] * 4
+    scratch += [dma((2, n, PIECES + 1))] * 4 + [dma((n_rows, 2))] * 2 + [dma((n_cols,))] * 2
+    scratch += [dma((n_rows,))] * 4 + [dma((3,))]
     out = pl.pallas_call(
         functools.partial(kernel, n_rows, n_cols),
         out_shape=jax.ShapeDtypeStruct((k, share), f32),
-        in_specs=[VMEM_SPEC] * 3,
+        in_specs=[ANY_SPEC, VMEM_SPEC, ANY_SPEC],
         out_specs=VMEM_SPEC,
         scratch_shapes=scratch,
         compiler_params=pltpu.CompilerParams(

time: 33.1 us -> 32.5 us (0.982)
  Pallas kernels: 31.5 us -> 30.8 us
    pallas_call x1, Pallas kernels: 31.5 us -> 30.8 us  [local(): pl.pallas_call(functools.partial(kernel, n_rows, n_cols), out_shape=jax.S...]
where the time goes in v4:
time: 32.5 us; the launch traced here: 32.3 us
  Pallas kernels  30.8 us (95%)
  local copies, waits for them, and re-layouts  1.47 us (5%)
    pallas_call x1, Pallas kernels, local(): pl.pallas_call(functools.partial(kernel, n_rows, n_cols), out_shape=jax.S...  30.8 us
    unnamed x1, local copies, waits for them, and re-layouts  1.47 us

profile of v4, /device:TPU:0, one launch (start us, length us, event | category | flops | bytes accessed | tf_op | source)
XLA Modules:
  0.0 32.3 jit_solution(17395786646298058539)
XLA Ops:
  0.0 30.8 %shard_map.37 = f32[64,256]{1,0:T(8,128)} custom-call(bf16[256,256]{1,0:T(8,128)(2,1)} %pts_ref.1, f32[1,256]{1,0:T(1,128)} %bitcast.5, bf16[64,256]{1,0:T(8,128)(2,1)} %bitcast.4), custom_call_target="tpu_custom_call" | custom-call | tf_op jit(solution)/shard_map/pallas_call | solution.py:376
  30.8 1.5 %copy.5 = f32[256,64]{0,1:T(8,128)} copy(f32[256,64]{0,1:T(8,128)} %bitcast.3) | data formatting | bytes 131072
